TPU v7x, 256 devices: a whole 4x4x8 slice. The times are simulated.
256 devices in a mesh: dp: 8 (over y, core), expert: 32 (over x, z).
Axes of the slice: x: 4, y: 4, z: 8, core: 2. Of those that a mesh axis runs over, the one named last changes fastest.
Arguments:
- tokens: bfloat16 [32768, 3072], P(('dp', 'expert')), may hold values from -6 to 6
- cotangent: bfloat16 [32768, 3072], P(('dp', 'expert')), may hold values from -0.3125 to 0.3125
- route_ids: int32 [32768, 2], P(('dp', 'expert')), may hold values from 0 to 7, all different within a row; in each aligned block of 128 rows (0 to 127, 128 to 255, ...) at most 36 rows name the same one
- route_probs: float32 [32768, 2], P(('dp', 'expert')), may hold values from 0.2 to 1
- gate_weight: bfloat16 [3072, 8192], P(None, 'expert'), may hold values from -0.109375 to 0.109375
- up_weight: bfloat16 [3072, 8192], P(None, 'expert'), may hold values from -0.109375 to 0.109375
- down_weight: bfloat16 [8192, 3072], P('expert'), may hold values from -0.0625 to 0.0625
Outputs:
- token_grad: bfloat16 [32768, 3072], P(('dp', 'expert'))
- gate_grad: bfloat16 [3072, 8192], P('dp', 'expert')
- up_grad: bfloat16 [3072, 8192], P('dp', 'expert')
- down_grad: bfloat16 [8192, 3072], P('expert', 'dp')
Inputs may be any that keep to these rules, and one draw needn't show every extreme that they name: `route_ids`: in every block of 128 consecutive tokens (the tokens of one device) at most 36 tokens name any one expert, a bound that some block reaches; a token's 2 ids differ.
All inputs are finite; a program needn't handle non-finite values.
Results may differ from a plain program's by a relative error of at most 0.023.
Values may be sent and summed in bfloat16 or wider, within the bound.
A program may use at most 128 MiB of HBM per device.

v0:
```python
import jax
import jax.numpy as jnp
from jax import lax
from jax.sharding import PartitionSpec as P

CAP = 36


def pick_rows(placer, values):
    return lax.dot_general(
        placer, values, (((0,), (0,)), ((), ())), preferred_element_type=jnp.float32
    ).astype(jnp.bfloat16)


def per_device(tokens, cotangent, route_ids, route_probs, gate_weight, up_weight, down_weight):
    hits = route_ids == 0
    chosen = jnp.any(hits, axis=1).astype(jnp.int32)
    share = jnp.sum(jnp.where(hits, route_probs, 0.0), axis=1)
    slots = jnp.cumsum(chosen) - chosen
    placer_mask = (slots[:, None] == jnp.arange(CAP, dtype=jnp.int32)[None, :]) & (
        chosen[:, None] == 1
    )
    placer = placer_mask.astype(jnp.float32)
    placer_half = placer_mask.astype(jnp.bfloat16)
    local_rows = pick_rows(placer_half, tokens)
    local_cotan = pick_rows(placer_half, cotangent)
    local_shares = jnp.sum(placer * share[:, None], axis=0)
    routed, routed_cotan, routed_shares = (
        lax.all_gather(local_rows, "expert", axis=0, tiled=True),
        lax.all_gather(local_cotan, "expert", axis=0, tiled=True),
        lax.all_gather(local_shares.astype(jnp.bfloat16), "expert", axis=0, tiled=True).astype(
            local_shares.dtype
        ),
    )
    gate_pre = jnp.dot(routed, gate_weight, preferred_element_type=jnp.float32)
    up_pre = jnp.dot(routed, up_weight, preferred_element_type=jnp.float32)
    sigma = jax.nn.sigmoid(gate_pre)
    gate_act = gate_pre * sigma
    hidden = (gate_act * up_pre).astype(jnp.bfloat16)
    gate_pre, up_pre, sigma, gate_act, hidden = (gate_pre, up_pre, sigma, gate_act, hidden)
    scaled = (routed_shares[:, None] * routed_cotan.astype(jnp.float32)).astype(jnp.bfloat16)
    down_part = lax.dot_general(
        hidden, scaled, (((0,), (0,)), ((), ())), preferred_element_type=jnp.float32
    )
    hidden_back = lax.dot_general(
        scaled, down_weight, (((1,), (1,)), ((), ())), preferred_element_type=jnp.float32
    )
    gate_back = (hidden_back * up_pre * sigma * (1.0 + gate_pre * (1.0 - sigma))).astype(
        jnp.bfloat16
    )
    up_back = (hidden_back * gate_act).astype(jnp.bfloat16)
    gate_part = lax.dot_general(
        routed, gate_back, (((0,), (0,)), ((), ())), preferred_element_type=jnp.float32
    )
    up_part = lax.dot_general(
        routed, up_back, (((0,), (0,)), ((), ())), preferred_element_type=jnp.float32
    )
    gate_sum, up_sum, down_sum = (
        lax.psum_scatter(
            gate_part.astype(jnp.bfloat16), "dp", scatter_dimension=0, tiled=True
        ).astype(jnp.float32),
        lax.psum_scatter(
            up_part.astype(jnp.bfloat16), "dp", scatter_dimension=0, tiled=True
        ).astype(jnp.float32),
        lax.psum_scatter(
            down_part.astype(jnp.bfloat16), "dp", scatter_dimension=1, tiled=True
        ).astype(jnp.float32),
    )
    partial_value = lax.dot_general(
        gate_back, gate_weight, (((1,), (1,)), ((), ())), preferred_element_type=jnp.float32
    )
    partial_value = partial_value + lax.dot_general(
        up_back, up_weight, (((1,), (1,)), ((), ())), preferred_element_type=jnp.float32
    )
    returned = lax.psum_scatter(
        partial_value.astype(jnp.bfloat16), "expert", scatter_dimension=0, tiled=True
    ).astype(jnp.float32)
    token_grad = jnp.dot(placer, returned, precision=lax.Precision.HIGHEST).astype(jnp.bfloat16)
    return (
        token_grad,
        gate_sum.astype(jnp.bfloat16),
        up_sum.astype(jnp.bfloat16),
        down_sum.astype(jnp.bfloat16),
    )


def solution(mesh):
    in_specs = (
        P(("dp", "expert"), None),
        P(("dp", "expert"), None),
        P(("dp", "expert"), None),
        P(("dp", "expert"), None),
        P(None, "expert"),
        P(None, "expert"),
        P("expert", None),
    )
    out_specs = (P(("dp", "expert"), None), P("dp", "expert"), P("dp", "expert"), P("expert", "dp"))
    return jax.shard_map(
        per_device, mesh=mesh, in_specs=in_specs, out_specs=out_specs, check_vma=False
    )
```

profile of v0, /device:TPU:2, one launch (start us, length us, event | category | flops | bytes accessed | tf_op | source)
XLA Modules:
  0.0 405.0 jit_solution(14300400901029948780)
XLA Ops:
  7.2 0.0 copy-start
  7.2 0.0 copy-start.9
  7.2 0.0 all-gather.7.cloned.1.call-start
  7.3 0.8 fusion.18
  8.1 0.1 copy.14
  8.2 0.2 reduce-window.8
  8.4 0.1 reduce
  8.5 2.1 fusion.3
  10.6 0.0 all-gather.7.cloned.1.call-update
  10.6 0.0 all-gather.5.cloned.1.call-start
  10.7 0.9 fusion.2
  11.6 0.0 all-gather.5.cloned.1.call-update
  11.6 0.0 reduce-scatter.12.cloned.1.call-start
  11.7 0.6 fusion.21
  13.0 0.1 select_reduce_fusion
  13.1 0.2 dynamic-update-slice
  13.4 66.5 %all-reduce = bf16[1152]{0:T(1024)(128)(2,1)S(1)} all-reduce(bf16[1152]{0:T(1024)(128)(2,1)S(1)} %dynamic-update-slice), channel_id=1, replica_groups=mesh['dp'=8,'expert'=32] {'expert'}, use_global_device_ids=true, to_apply=%add | all-reduce | flops 1152 | bytes 4608
  79.9 28.5 %all-gather.7.cloned.1.call-done = bf16[32,36,3072]{2,1,0:T(8,128)(2,1)} async-done(((bf16[1,36,3072]{2,1,0:T(8,128)(2,1)}), bf16[32,36,3072]{2,1,0:T(8,128)(2,1)}) %all-gather.7.cloned.1.call-update) | async-done | bytes 7077904 | tf_op jit(solution)/shard_map/all_gather | solution.py:29
  108.4 8.8 %reshape.52 = bf16[1152,3072]{1,0:T(8,128)(2,1)} reshape(bf16[32,36,3072]{2,1,0:T(8,128)(2,1)} %all-gather.7.cloned.1.call-done) | data formatting | bytes 14155776
  117.2 6.2 %fusion.23 = f32[1152,256]{1,0:T(8,128)} fusion(bf16[1152,3072]{1,0:T(8,128)(2,1)} %reshape.52, bf16[3072,256]{1,0:T(8,128)(2,1)S(1)} %copy-done), kind=kOutput, calls=%fused_computation.37 | convolution fusion | flops 1811939328 | bytes 9830400 | tf_op jit(solution)/shard_map/dot_general | solution.py:35
  123.4 3.0 fusion.22
  126.5 76.7 %all-gather.5.cloned.1.call-done = bf16[32,36,3072]{2,1,0:T(8,128)(2,1)} async-done(((bf16[1,36,3072]{2,1,0:T(8,128)(2,1)}), bf16[32,36,3072]{2,1,0:T(8,128)(2,1)}) %all-gather.5.cloned.1.call-update) | async-done | bytes 7077904 | tf_op jit(solution)/shard_map/all_gather | solution.py:30
  203.2 9.8 %reshape.53 = f32[1152,3072]{1,0:T(8,128)} reshape(bf16[32,36,3072]{2,1,0:T(8,128)(2,1)} %all-gather.5.cloned.1.call-done) | data formatting | bytes 21233664 | tf_op jit(solution)/shard_map/convert_element_type | solution.py:41
  213.0 8.2 %convolution_convert_fusion = bf16[256,3072]{1,0:T(8,128)(2,1)S(1)} fusion(f32[1152,256]{1,0:T(8,128)} %fusion.22, f32[1152,256]{1,0:T(8,128)} %fusion.23, f32[1152,3072]{1,0:T(8,128)} %reshape.53, f32[1152]{0:T(1024)S(1)} %convert_element_type.76), kind=kOutput, calls=%fused_computation.3 | convolution fusion | flops 1821573120 | bytes 18092544 | tf_op jit(solution)/shard_map/dot_general | solution.py:42
  221.2 1.6 copy.15
  222.8 0.0 reduce-scatter.12.cloned.1.call-update
  222.8 0.2 reduce-scatter.8.cloned.1.call-start
  223.1 1.0 copy-done.4
  224.1 9.0 %multiply_convert_fusion.2 = (bf16[1152,256]{1,0:T(8,128)(2,1)}, bf16[1152,256]{1,0:T(8,128)(2,1)S(1)}) fusion(f32[1152,256]{1,0:T(8,128)S(1)} %copy-done.4, f32[1152,256]{1,0:T(8,128)} %fusion.22, bf16[256,3072]{1,0:T(8,128)(2,1)} %param.13, f32[1152,3072]{1,0:T(8,128)} %reshape.53, f32[1152]{0:T(1024)S(1)} %convert_element_type.76), kind=kOutput, calls=%fused_computation.12 | convolution fusion | flops 1822851072 | bytes 19272192 | tf_op jit(solution)/shard_map/dot_general | solution.py:45
  233.1 6.5 %convolution_convert_fusion.2 = bf16[3072,256]{1,0:T(8,128)(2,1)} fusion(bf16[1152,3072]{1,0:T(8,128)(2,1)} %reshape.52, bf16[1152,256]{1,0:T(8,128)(2,1)S(1)} %get-tuple-element.5), kind=kOutput, calls=%fused_computation.5 | convolution fusion | flops 1812725760 | bytes 9240576 | tf_op jit(solution)/shard_map/dot_general | solution.py:52
  239.6 0.0 reduce-scatter.8.cloned.1.call-update
  239.6 0.0 reduce-scatter.10.cloned.1.call-start
  239.6 0.0 copy-start.6
  239.6 7.1 %fusion.24 = f32[1152,3072]{1,0:T(8,128)} fusion(bf16[1152,256]{1,0:T(8,128)(2,1)S(1)} %get-tuple-element.5, bf16[3072,256]{1,0:T(8,128)(2,1)S(1)} %copy-done), kind=kOutput, calls=%fused_computation.38 | convolution fusion | flops 1811939328 | bytes 16318464 | tf_op jit(solution)/shard_map/dot_general | solution.py:69
  246.7 6.5 %convolution_convert_fusion.1 = bf16[3072,256]{1,0:T(8,128)(2,1)} fusion(bf16[1152,3072]{1,0:T(8,128)(2,1)} %reshape.52, bf16[1152,256]{1,0:T(8,128)(2,1)S(1)} %copy-done.6), kind=kOutput, calls=%fused_computation.4 | convolution fusion | flops 1812725760 | bytes 9240576 | tf_op jit(solution)/shard_map/dot_general | solution.py:55
  253.3 10.3 %fusion.1 = bf16[1152,3072]{1,0:T(8,128)(2,1)} fusion(f32[1152,3072]{1,0:T(8,128)} %fusion.24, bf16[1152,256]{1,0:T(8,128)(2,1)} %get-tuple-element.4, bf16[3072,256]{1,0:T(8,128)(2,1)S(1)} %copy-done.3), kind=kOutput, calls=%fused_computation.2 | convolution fusion | flops 1819017216 | bytes 23396352 | tf_op jit(solution)/shard_map/dot_general | solution.py:72
  263.5 0.0 reduce-scatter.10.cloned.1.call-update
  263.6 92.1 %fusion = bf16[40,3072]{1,0:T(8,128)(2,1)S(1)} fusion(bf16[1152,3072]{1,0:T(8,128)(2,1)} %fusion.1), kind=kCustom, calls=%all-reduce-scatter | all-reduce-scatter fusion | flops 3932161 | bytes 7324672
  355.7 1.9 collective-permute-start.2
  357.6 5.4 %collective-permute-start.1 = (bf16[40,3072]{1,0:T(8,128)(2,1)S(1)}, bf16[40,3072]{1,0:T(8,128)(2,1)S(1)}, u32[]{:S(2)}, u32[]{:S(2)}) collective-permute-start(bf16[40,3072]{1,0:T(8,128)(2,1)S(1)} %fusion), channel_id=1, source_target_pairs={{0,2},{1,3},{2,4},{3,5},{4,6},{5,7},{6,8},{7,9},{8,10},{9,11},{10,... | collective-permute-start | bytes 737288
  363.1 1.9 collective-permute-start
  365.0 6.0 %collective-permute-start.3 = (bf16[4,3072]{1,0:T(4,128)(2,1)S(1)}, bf16[4,3072]{1,0:T(4,128)(2,1)S(1)}, u32[]{:S(2)}, u32[]{:S(2)}) collective-permute-start(bf16[4,3072]{1,0:T(4,128)(2,1)S(1)} %slice), channel_id=1, source_target_pairs={{0,4},{1,5},{2,6},{3,7},{4,8},{5,9},{6,10},{7,11},{8,12},{9,13},{1... | collective-permute-start | bytes 73736
  371.7 20.6 %collective-permute-done.3 = bf16[4,3072]{1,0:T(4,128)(2,1)S(1)} collective-permute-done((bf16[4,3072]{1,0:T(4,128)(2,1)S(1)}, bf16[4,3072]{1,0:T(4,128)(2,1)S(1)}, u32[]{:S(2)}, u32[]{:S(2)}) %collective-permute-start.3) | collective-permute-done | bytes 24608
  392.3 0.0 collective-permute-done.2
  392.3 0.0 collective-permute-done.1
  392.3 3.1 concatenate
  395.4 1.3 convolution_convert_fusion.3
  396.7 1.7 copy.16
  (26 shorter events, 0.1 us)
Async XLA Ops:
  7.2 110.0 %copy-start = (bf16[3072,256]{1,0:T(8,128)(2,1)S(1)}, bf16[3072,256]{1,0:T(8,128)(2,1)}, u32[]{:S(2)}) copy-start(bf16[3072,256]{1,0:T(8,128)(2,1)} %param.11) | copy-start | bytes 4718596
  7.2 4.5 %copy-start.9 = (u32[256]{0:T(256)S(1)}, u32[256]{0:T(256)}, u32[]{:S(2)}) copy-start(u32[256]{0:T(256)} %constant.20) | copy-start | bytes 3076
  7.2 5.7 %copy-start.7 = (s32[128,2]{0,1:T(2,128)S(1)}, s32[128,2]{0,1:T(2,128)}, u32[]{:S(2)}) copy-start(s32[128,2]{0,1:T(2,128)} %param.9) | copy-start | bytes 3076
  7.2 3.5 copy-start.5
  7.2 5.7 %copy-start.8 = (f32[128,2]{0,1:T(2,128)S(1)}, f32[128,2]{0,1:T(2,128)}, u32[]{:S(2)}) copy-start(f32[128,2]{0,1:T(2,128)} %param.10) | copy-start | bytes 3076
  7.2 101.2 %all-gather.7.cloned.1.call-start = ((), (), s32[]{:S(2)}) async-start(), calls=%async_computation.6 | async-start | bytes 8110080 | tf_op jit(solution)/shard_map/all_gather | solution.py:29
  10.6 192.6 %all-gather.5.cloned.1.call-start = ((), (), s32[]{:S(2)}) async-start(), calls=%async_computation.5 | async-start | bytes 8110080 | tf_op jit(solution)/shard_map/all_gather | solution.py:30
  11.6 385.1 %reduce-scatter.12.cloned.1.call-start = ((), (), s32[]{:S(2)}) async-start(), calls=%async_computation.7 | async-start | bytes 1769472
  117.2 6.2 %copy-start.1 = (bf16[1152,3072]{1,0:T(8,128)(2,1)S(1)}, bf16[1152,3072]{1,0:T(8,128)(2,1)}, u32[]{:S(2)}) copy-start(bf16[1152,3072]{1,0:T(8,128)(2,1)} %reshape.52) | copy-start | bytes 21233668
  117.2 6.2 %copy-start.2 = (bf16[3072,256]{1,0:T(8,128)(2,1)S(1)}, bf16[3072,256]{1,0:T(8,128)(2,1)}, u32[]{:S(2)}) copy-start(bf16[3072,256]{1,0:T(8,128)(2,1)} %param.12) | copy-start | bytes 4718596
  222.8 1.3 copy-start.4
  222.8 175.6 %reduce-scatter.8.cloned.1.call-start = ((), (), s32[]{:S(2)}) async-start(), calls=%async_computation.3 | async-start | bytes 1769472 | tf_op jit(solution)/shard_map/reduce_scatter | solution.py:59
  239.6 158.9 %reduce-scatter.10.cloned.1.call-start = ((), (), s32[]{:S(2)}) async-start(), calls=%async_computation.4 | async-start | bytes 1769472 | tf_op jit(solution)/shard_map/reduce_scatter | solution.py:62
  239.6 7.1 %copy-start.6 = (bf16[1152,256]{1,0:T(8,128)(2,1)S(1)}, bf16[1152,256]{1,0:T(8,128)(2,1)}, u32[]{:S(2)}) copy-start(bf16[1152,256]{1,0:T(8,128)(2,1)} %get-tuple-element.4) | copy-start | bytes 1769476
  246.7 6.5 %copy-start.3 = (bf16[3072,256]{1,0:T(8,128)(2,1)S(1)}, bf16[3072,256]{1,0:T(8,128)(2,1)}, u32[]{:S(2)}) copy-start(bf16[3072,256]{1,0:T(8,128)(2,1)} %param.12) | copy-start | bytes 4718596
  355.7 36.6 %collective-permute-start.2 = (bf16[40,3072]{1,0:T(8,128)(2,1)S(1)}, bf16[40,3072]{1,0:T(8,128)(2,1)S(1)}, u32[]{:S(2)}, u32[]{:S(2)}) collective-permute-start(bf16[40,3072]{1,0:T(8,128)(2,1)S(1)} %fusion), channel_id=1, source_target_pairs={{0,3},{1,4},{2,5},{3,6},{4,7},{5,8},{6,9},{7,10},{8,11},{9,12},{10... | collective-permute-start | bytes 737288
  357.6 34.7 %collective-permute-start.1 = (bf16[40,3072]{1,0:T(8,128)(2,1)S(1)}, bf16[40,3072]{1,0:T(8,128)(2,1)S(1)}, u32[]{:S(2)}, u32[]{:S(2)}) collective-permute-start(bf16[40,3072]{1,0:T(8,128)(2,1)S(1)} %fusion), channel_id=1, source_target_pairs={{0,2},{1,3},{2,4},{3,5},{4,6},{5,7},{6,8},{7,9},{8,10},{9,11},{10,... | collective-permute-start | bytes 737288
  363.1 29.3 %collective-permute-start = (bf16[40,3072]{1,0:T(8,128)(2,1)S(1)}, bf16[40,3072]{1,0:T(8,128)(2,1)}, u32[]{:S(2)}, u32[]{:S(2)}) collective-permute-start(bf16[40,3072]{1,0:T(8,128)(2,1)S(1)} %fusion), channel_id=1, source_target_pairs={{0,1},{1,2},{2,3},{3,4},{4,5},{5,6},{6,7},{7,8},{8,9},{9,10},{10,1... | collective-permute-start | bytes 737288
  365.0 27.3 %collective-permute-start.3 = (bf16[4,3072]{1,0:T(4,128)(2,1)S(1)}, bf16[4,3072]{1,0:T(4,128)(2,1)S(1)}, u32[]{:S(2)}, u32[]{:S(2)}) collective-permute-start(bf16[4,3072]{1,0:T(4,128)(2,1)S(1)} %slice), channel_id=1, source_target_pairs={{0,4},{1,5},{2,6},{3,7},{4,8},{5,9},{6,10},{7,11},{8,12},{9,13},{1... | collective-permute-start | bytes 73736
Sparse Core Ops, SparseCore 0:
  11.2 97.2 all-gather.6
  111.0 92.1 all-gather.4
  223.0 33.8 reduce-scatter.11
  259.9 34.9 reduce-scatter.7
  297.9 34.9 reduce-scatter.9
where the time goes:
time: 406 us; the launch traced here: 405 us
  blocking collectives  159 us (39%)
  waiting for transfers between devices  126 us (31%)
  matrix products  61.1 us (15%)
  local copies, waits for them, and re-layouts  27.1 us (7%)
  starting transfers between devices  15.7 us (4%)
  between operations  15.3 us (4%)
    unnamed x2, blocking collectives  159 us
    all_gather x1, waiting for transfers between devices, per_device(): lax.all_gather(local_cotan, 'expert', axis=0, tiled=True)  76.7 us
    all_gather x1, waiting for transfers between devices, per_device(): lax.all_gather(local_rows, 'expert', axis=0, tiled=True)  28.5 us
    unnamed x10, waiting for transfers between devices  20.7 us
    unnamed x28, local copies, waits for them, and re-layouts  17.2 us
    unnamed x5, starting transfers between devices  15.4 us
    dot_general x1, matrix products, per_device(): lax.dot_general(up_back, up_weight, (((1,), (1,)), ((), ())), preferred_e...  10.3 us
    convert_element_type x1, local copies, waits for them, and re-layouts, per_device(): routed_cotan.astype(jnp.float32)  9.83 us
  transfers between devices with their start and end apart: 9, of which 3 were waited for; matrix products, arithmetic and copies ran while one was open for 39% of the time, Pallas kernels for 0%

commit v1 on v0

--- a/solution.py
+++ b/solution.py
@@ -27,7 +27,10 @@
     local_shares = jnp.sum(placer * share[:, None], axis=0)
     routed, routed_cotan, routed_shares = (
         lax.all_gather(local_rows, "expert", axis=0, tiled=True),
-        lax.all_gather(local_cotan, "expert", axis=0, tiled=True),
+        jnp.concatenate(
+            lax.all_to_all(jnp.stack([local_cotan] * lax.axis_size("expert")), "expert", 0, 0),
+            axis=0,
+        ),
         lax.all_gather(local_shares.astype(jnp.bfloat16), "expert", axis=0, tiled=True).astype(
             local_shares.dtype
         ),

time: 406 us -> 526 us (1.30)
  blocking collectives: 159 us -> 374 us
  waiting for transfers between devices: 126 us -> 19 us
  starting transfers between devices: 15.7 us -> 24.4 us
    unnamed x2, blocking collectives: 159 us -> 374 us
    all_gather x1 -> x0, waiting for transfers between devices: 76.7 us -> none  [per_device(): lax.all_gather(local_cotan, 'expert', axis=0, tiled=True)]
    all_gather x1, waiting for transfers between devices: 28.5 us -> 0.02 us  [per_device(): lax.all_gather(local_rows, 'expert', axis=0, tiled=True)]
    all_to_all x0 -> x1, starting transfers between devices: none -> 11.8 us  [per_device(): lax.all_to_all(jnp.stack([local_cotan] * lax.axis_size('expert')), 'exper...]
    unnamed x10 -> x9, waiting for transfers between devices: 20.7 us -> 18.9 us
  transfers between devices with their start and end apart: 9 -> 9, of which waited for: 3 -> 1; matrix products, arithmetic and copies ran while one was open for 39% -> 32% of each run, Pallas kernels for 0% -> 0%
where the time goes in v1:
time: 526 us; the launch traced here: 525 us
  blocking collectives  374 us (71%)
  matrix products  60.4 us (11%)
  local copies, waits for them, and re-layouts  31.2 us (6%)
  starting transfers between devices  24.4 us (5%)
  waiting for transfers between devices  19 us (4%)
  between operations  15.3 us (3%)
    unnamed x2, blocking collectives  374 us
    unnamed x9, waiting for transfers between devices  18.9 us
    unnamed x28, local copies, waits for them, and re-layouts  17.2 us
    unnamed x5, starting transfers between devices  12.3 us
    all_to_all x1, starting transfers between devices, per_device(): lax.all_to_all(jnp.stack([local_cotan] * lax.axis_size('expert')), 'exper...  11.8 us
  transfers between devices with their start and end apart: 9, of which 1 were waited for; matrix products, arithmetic and copies ran while one was open for 32% of the time, Pallas kernels for 0%

profile of v1, /device:TPU:2, one launch (start us, length us, event | category | flops | bytes accessed | tf_op | source)
XLA Modules:
  0.0 525.4 jit_solution(720912404559800143)
XLA Ops:
  7.2 0.0 copy-start
  7.2 0.0 all-gather.3.cloned.1.call-start
  7.2 0.8 fusion.17
  8.1 0.1 copy.14
  8.2 0.2 reduce-window.8
  8.4 0.1 reduce
  8.5 2.1 fusion.2
  10.6 0.0 all-gather.3.cloned.1.call-update
  10.6 0.2 convolution_convert_fusion.5
  10.9 4.0 stack.2
  14.9 11.8 %all-to-all-start = ((bf16[32,36,3072]{2,1,0:T(8,128)(2,1)}), bf16[32,36,3072]{2,1,0:T(8,128)(2,1)}, u32[]{:S(2)}, u32[]{:S(2)}) async-start(bf16[32,36,3072]{2,1,0:T(8,128)(2,1)} %stack.2), calls=%async_computation | async-start | bytes 15728640 | tf_op jit(solution)/shard_map/all_to_all | solution.py:31
  26.7 0.0 reduce-scatter.12.cloned.1.call-start
  26.8 0.6 fusion.20
  28.1 0.1 select_reduce_fusion
  28.2 0.2 dynamic-update-slice
  28.4 272.4 %all-reduce = bf16[1152]{0:T(1024)(128)(2,1)S(1)} all-reduce(bf16[1152]{0:T(1024)(128)(2,1)S(1)} %dynamic-update-slice), channel_id=1, replica_groups=mesh['dp'=8,'expert'=32] {'expert'}, use_global_device_ids=true, to_apply=%add | all-reduce | flops 1152 | bytes 4608
  300.9 0.0 all-gather.3.cloned.1.call-done
  300.9 8.8 %reshape.56 = bf16[1152,3072]{1,0:T(8,128)(2,1)} reshape(bf16[32,36,3072]{2,1,0:T(8,128)(2,1)} %all-gather.3.cloned.1.call-done) | data formatting | bytes 14155776
  309.7 6.2 %fusion.22 = f32[1152,256]{1,0:T(8,128)} fusion(bf16[1152,3072]{1,0:T(8,128)(2,1)} %reshape.56, bf16[3072,256]{1,0:T(8,128)(2,1)S(1)} %copy-done), kind=kOutput, calls=%fused_computation.36 | convolution fusion | flops 1811939328 | bytes 9830400 | tf_op jit(solution)/shard_map/dot_general | solution.py:38
  315.9 3.0 fusion.21
  318.9 0.0 all-to-all-done
  319.0 9.8 %reshape.51 = f32[1152,3072]{1,0:T(8,128)} reshape(bf16[32,36,3072]{2,1,0:T(8,128)(2,1)} %all-to-all-done) | data formatting | bytes 21233664 | tf_op jit(solution)/shard_map/convert_element_type | solution.py:44
  328.8 8.2 %convolution_convert_fusion = bf16[256,3072]{1,0:T(8,128)(2,1)S(1)} fusion(f32[1152,256]{1,0:T(8,128)} %fusion.21, f32[1152,256]{1,0:T(8,128)} %fusion.22, f32[1152,3072]{1,0:T(8,128)} %reshape.51, f32[1152]{0:T(1024)S(1)} %convert_element_type.79), kind=kOutput, calls=%fused_computation.3 | convolution fusion | flops 1821573120 | bytes 18092544 | tf_op jit(solution)/shard_map/dot_general | solution.py:45
  337.0 1.6 copy.15
  338.6 0.0 reduce-scatter.12.cloned.1.call-update
  338.6 0.2 reduce-scatter.8.cloned.1.call-start
  338.9 1.0 copy-done.4
  339.9 9.0 %multiply_convert_fusion.2 = (bf16[1152,256]{1,0:T(8,128)(2,1)}, bf16[1152,256]{1,0:T(8,128)(2,1)S(1)}) fusion(f32[1152,256]{1,0:T(8,128)S(1)} %copy-done.4, f32[1152,256]{1,0:T(8,128)} %fusion.21, bf16[256,3072]{1,0:T(8,128)(2,1)} %param.13, f32[1152,3072]{1,0:T(8,128)} %reshape.51, f32[1152]{0:T(1024)S(1)} %convert_element_type.79), kind=kOutput, calls=%fused_computation.11 | convolution fusion | flops 1822851072 | bytes 19272192 | tf_op jit(solution)/shard_map/dot_general | solution.py:48
  348.9 6.5 %convolution_convert_fusion.2 = bf16[3072,256]{1,0:T(8,128)(2,1)} fusion(bf16[1152,3072]{1,0:T(8,128)(2,1)} %reshape.56, bf16[1152,256]{1,0:T(8,128)(2,1)S(1)} %get-tuple-element.5), kind=kOutput, calls=%fused_computation.5 | convolution fusion | flops 1812725760 | bytes 9240576 | tf_op jit(solution)/shard_map/dot_general | solution.py:55
  355.3 0.0 reduce-scatter.8.cloned.1.call-update
  355.4 0.0 reduce-scatter.10.cloned.1.call-start
  355.4 0.0 copy-start.6
  355.4 7.1 %fusion.23 = f32[1152,3072]{1,0:T(8,128)} fusion(bf16[1152,256]{1,0:T(8,128)(2,1)S(1)} %get-tuple-element.5, bf16[3072,256]{1,0:T(8,128)(2,1)S(1)} %copy-done), kind=kOutput, calls=%fused_computation.37 | convolution fusion | flops 1811939328 | bytes 16318464 | tf_op jit(solution)/shard_map/dot_general | solution.py:72
  362.5 6.5 %convolution_convert_fusion.1 = bf16[3072,256]{1,0:T(8,128)(2,1)} fusion(bf16[1152,3072]{1,0:T(8,128)(2,1)} %reshape.56, bf16[1152,256]{1,0:T(8,128)(2,1)S(1)} %copy-done.6), kind=kOutput, calls=%fused_computation.4 | convolution fusion | flops 1812725760 | bytes 9240576 | tf_op jit(solution)/shard_map/dot_general | solution.py:58
  369.0 10.3 %fusion.1 = bf16[1152,3072]{1,0:T(8,128)(2,1)} fusion(f32[1152,3072]{1,0:T(8,128)} %fusion.23, bf16[1152,256]{1,0:T(8,128)(2,1)} %get-tuple-element.4, bf16[3072,256]{1,0:T(8,128)(2,1)S(1)} %copy-done.3), kind=kOutput, calls=%fused_computation.2 | convolution fusion | flops 1819017216 | bytes 23396352 | tf_op jit(solution)/shard_map/dot_general | solution.py:75
  379.3 0.0 reduce-scatter.10.cloned.1.call-update
  379.4 101.5 %fusion = bf16[40,3072]{1,0:T(8,128)(2,1)S(1)} fusion(bf16[1152,3072]{1,0:T(8,128)(2,1)} %fusion.1), kind=kCustom, calls=%all-reduce-scatter | all-reduce-scatter fusion | flops 3932161 | bytes 7324672
  480.8 1.9 collective-permute-start.2
  482.8 1.9 collective-permute-start.1
  484.7 1.9 collective-permute-start
  486.7 6.5 %collective-permute-start.3 = (bf16[4,3072]{1,0:T(4,128)(2,1)S(1)}, bf16[4,3072]{1,0:T(4,128)(2,1)S(1)}, u32[]{:S(2)}, u32[]{:S(2)}) collective-permute-start(bf16[4,3072]{1,0:T(4,128)(2,1)S(1)} %slice), channel_id=1, source_target_pairs={{0,4},{1,5},{2,6},{3,7},{4,8},{5,9},{6,10},{7,11},{8,12},{9,13},{1... | collective-permute-start | bytes 73736
  493.8 18.9 %collective-permute-done.3 = bf16[4,3072]{1,0:T(4,128)(2,1)S(1)} collective-permute-done((bf16[4,3072]{1,0:T(4,128)(2,1)S(1)}, bf16[4,3072]{1,0:T(4,128)(2,1)S(1)}, u32[]{:S(2)}, u32[]{:S(2)}) %collective-permute-start.3) | collective-permute-done | bytes 24608
  512.7 0.0 collective-permute-done.2
  512.7 0.0 collective-permute-done.1
  512.7 0.0 collective-permute-done
  512.7 3.1 concatenate
  515.8 1.3 convolution_convert_fusion.3
  517.1 1.7 copy.16
  (26 shorter events, 0.1 us)
Async XLA Ops:
  7.2 302.5 %copy-start = (bf16[3072,256]{1,0:T(8,128)(2,1)S(1)}, bf16[3072,256]{1,0:T(8,128)(2,1)}, u32[]{:S(2)}) copy-start(bf16[3072,256]{1,0:T(8,128)(2,1)} %param.11) | copy-start | bytes 4718596
  7.2 3.4 copy-start.5
  7.2 293.7 %all-gather.3.cloned.1.call-start = ((), (), s32[]{:S(2)}) async-start(), calls=%async_computation.6 | async-start | bytes 8110080 | tf_op jit(solution)/shard_map/all_gather | solution.py:29
  14.9 11.9 %copy-start.9 = (u32[256]{0:T(256)S(1)}, u32[256]{0:T(256)}, u32[]{:S(2)}) copy-start(u32[256]{0:T(256)} %constant.20) | copy-start | bytes 3076
  14.9 13.1 %copy-start.7 = (s32[128,2]{0,1:T(2,128)S(1)}, s32[128,2]{0,1:T(2,128)}, u32[]{:S(2)}) copy-start(s32[128,2]{0,1:T(2,128)} %param.9) | copy-start | bytes 3076
  14.9 13.1 %copy-start.8 = (f32[128,2]{0,1:T(2,128)S(1)}, f32[128,2]{0,1:T(2,128)}, u32[]{:S(2)}) copy-start(f32[128,2]{0,1:T(2,128)} %param.10) | copy-start | bytes 3076
  14.9 304.1 %all-to-all-start = ((bf16[32,36,3072]{2,1,0:T(8,128)(2,1)}), bf16[32,36,3072]{2,1,0:T(8,128)(2,1)}, u32[]{:S(2)}, u32[]{:S(2)}) async-start(bf16[32,36,3072]{2,1,0:T(8,128)(2,1)} %stack.2), calls=%async_computation | async-start | bytes 15728640 | tf_op jit(solution)/shard_map/all_to_all | solution.py:31
  26.7 490.4 %reduce-scatter.12.cloned.1.call-start = ((), (), s32[]{:S(2)}) async-start(), calls=%async_computation.7 | async-start | bytes 1769472
  309.7 6.2 %copy-start.1 = (bf16[1152,3072]{1,0:T(8,128)(2,1)S(1)}, bf16[1152,3072]{1,0:T(8,128)(2,1)}, u32[]{:S(2)}) copy-start(bf16[1152,3072]{1,0:T(8,128)(2,1)} %reshape.56) | copy-start | bytes 21233668
  309.7 6.2 %copy-start.2 = (bf16[3072,256]{1,0:T(8,128)(2,1)S(1)}, bf16[3072,256]{1,0:T(8,128)(2,1)}, u32[]{:S(2)}) copy-start(bf16[3072,256]{1,0:T(8,128)(2,1)} %param.12) | copy-start | bytes 4718596
  338.6 1.3 copy-start.4
  338.6 180.2 %reduce-scatter.8.cloned.1.call-start = ((), (), s32[]{:S(2)}) async-start(), calls=%async_computation.4 | async-start | bytes 1769472 | tf_op jit(solution)/shard_map/reduce_scatter | solution.py:62
  355.4 163.5 %reduce-scatter.10.cloned.1.call-start = ((), (), s32[]{:S(2)}) async-start(), calls=%async_computation.5 | async-start | bytes 1769472 | tf_op jit(solution)/shard_map/reduce_scatter | solution.py:65
  355.4 7.1 %copy-start.6 = (bf16[1152,256]{1,0:T(8,128)(2,1)S(1)}, bf16[1152,256]{1,0:T(8,128)(2,1)}, u32[]{:S(2)}) copy-start(bf16[1152,256]{1,0:T(8,128)(2,1)} %get-tuple-element.4) | copy-start | bytes 1769476
  362.5 6.5 %copy-start.3 = (bf16[3072,256]{1,0:T(8,128)(2,1)S(1)}, bf16[3072,256]{1,0:T(8,128)(2,1)}, u32[]{:S(2)}) copy-start(bf16[3072,256]{1,0:T(8,128)(2,1)} %param.12) | copy-start | bytes 4718596
  480.8 31.9 %collective-permute-start.2 = (bf16[40,3072]{1,0:T(8,128)(2,1)S(1)}, bf16[40,3072]{1,0:T(8,128)(2,1)S(1)}, u32[]{:S(2)}, u32[]{:S(2)}) collective-permute-start(bf16[40,3072]{1,0:T(8,128)(2,1)S(1)} %fusion), channel_id=1, source_target_pairs={{0,3},{1,4},{2,5},{3,6},{4,7},{5,8},{6,9},{7,10},{8,11},{9,12},{10... | collective-permute-start | bytes 737288
  482.8 29.9 %collective-permute-start.1 = (bf16[40,3072]{1,0:T(8,128)(2,1)S(1)}, bf16[40,3072]{1,0:T(8,128)(2,1)S(1)}, u32[]{:S(2)}, u32[]{:S(2)}) collective-permute-start(bf16[40,3072]{1,0:T(8,128)(2,1)S(1)} %fusion), channel_id=1, source_target_pairs={{0,2},{1,3},{2,4},{3,5},{4,6},{5,7},{6,8},{7,9},{8,10},{9,11},{10,... | collective-permute-start | bytes 737288
  484.7 28.0 %collective-permute-start = (bf16[40,3072]{1,0:T(8,128)(2,1)S(1)}, bf16[40,3072]{1,0:T(8,128)(2,1)}, u32[]{:S(2)}, u32[]{:S(2)}) collective-permute-start(bf16[40,3072]{1,0:T(8,128)(2,1)S(1)} %fusion), channel_id=1, source_target_pairs={{0,1},{1,2},{2,3},{3,4},{4,5},{5,6},{6,7},{7,8},{8,9},{9,10},{10,1... | collective-permute-start | bytes 737288
  486.7 26.0 %collective-permute-start.3 = (bf16[4,3072]{1,0:T(4,128)(2,1)S(1)}, bf16[4,3072]{1,0:T(4,128)(2,1)S(1)}, u32[]{:S(2)}, u32[]{:S(2)}) collective-permute-start(bf16[4,3072]{1,0:T(4,128)(2,1)S(1)} %slice), channel_id=1, source_target_pairs={{0,4},{1,5},{2,6},{3,7},{4,8},{5,9},{6,10},{7,11},{8,12},{9,13},{1... | collective-permute-start | bytes 73736
Sparse Core Ops, SparseCore 0:
  11.1 201.3 all-gather.2
  338.8 39.8 reduce-scatter.11
  381.8 35.0 reduce-scatter.7
  419.9 34.9 reduce-scatter.9
